TPU v7x, 32 devices: a whole 2x2x4 slice. The times are simulated.
32 devices in a mesh: grp: 2 (over x), ep: 16 (over z, y, core).
Axes of the slice: x: 2, y: 2, z: 4, core: 2. Of those that a mesh axis runs over, the one named last changes fastest.
Arguments:
- tokens: bfloat16 [1024, 4096], P('ep'), may hold values from -6 to 6
- norm_gain: float32 [4096], replicated, may hold values from 0.1 to 1.9
- expert_ids: int32 [1024, 8], P('ep'), may hold values from 0 to 15, all different within a row; in each aligned block of 64 rows (0 to 63, 64 to 127, ...) at most 64 rows name the same one
- gate_scores: float32 [1024, 8], P('ep'), may hold values from 0.05 to 1
- w_gate: bfloat16 [16, 1536, 4096], P('ep', 'grp'), may hold values from -0.09375 to 0.09375
- w_up: bfloat16 [16, 1536, 4096], P('ep', 'grp'), may hold values from -0.09375 to 0.09375
- w_down: bfloat16 [16, 1536, 4096], P('ep', 'grp'), may hold values from -0.21875 to 0.21875
Outputs:
- moe_out: bfloat16 [1024, 4096], P('ep', 'grp')
Inputs may be any that keep to these rules, and one draw needn't show every extreme that they name: `expert_ids`: each row names 8 different experts. Within each aligned block of 64 rows (the rows of one device) no expert is named by more than 64 rows, and this bound is reached.
All inputs are finite; a program needn't handle non-finite values.
Results may differ from a plain program's by a relative error of at most 0.009.
Values may be sent and summed in bfloat16 or wider, within the bound.
A program may use at most 128 MiB of HBM per device.

v0:
```python
import jax
import jax.numpy as jnp
from jax import lax
from jax.sharding import PartitionSpec as P


def finish_expert(gate_proj, up_proj, w_down, sources, item_count, model_width):
    hidden = (jax.nn.silu(gate_proj) * up_proj).astype(jnp.bfloat16)
    outputs = jnp.dot(hidden, w_down[0], preferred_element_type=jnp.float32).astype(jnp.bfloat16)
    return outputs.reshape(sources, item_count, model_width)


def expert_block(received, w_gate, w_up, w_down):
    sources, item_count, model_width = received.shape
    flat_rows = received.reshape(sources * item_count, model_width)
    contract = (((1,), (1,)), ((), ()))
    gate_proj = lax.dot_general(flat_rows, w_gate[0], contract, preferred_element_type=jnp.float32)
    up_proj = lax.dot_general(flat_rows, w_up[0], contract, preferred_element_type=jnp.float32)
    return finish_expert(gate_proj, up_proj, w_down, sources, item_count, model_width)


def on_device(tokens, norm_gain, expert_ids, gate_scores, w_gate, w_up, w_down):
    experts = lax.axis_size("ep")
    tok_rows, model_width = tokens.shape
    top_count = expert_ids.shape[1]
    capacity = 2 * tok_rows * top_count // experts
    floated = tokens.astype(jnp.float32)
    scaled = lax.rsqrt(jnp.mean(floated * floated, axis=1, keepdims=True) + 1e-06)
    normed = (floated * scaled * norm_gain[None, :]).astype(jnp.bfloat16)
    mixing = gate_scores / jnp.sum(gate_scores, axis=1, keepdims=True)
    flat_ids = expert_ids.reshape(-1)
    onehot = (flat_ids[:, None] == jnp.arange(experts, dtype=jnp.int32)[None, :]).astype(jnp.int32)
    before = jnp.cumsum(onehot, axis=0) - onehot
    slot_rank = jnp.sum(before * onehot, axis=1)
    positions = flat_ids * capacity + slot_rank
    token_slots = positions.reshape(tok_rows, top_count)
    buckets = jnp.arange(experts * capacity, dtype=jnp.int32)
    routing = jnp.any(token_slots[None, :, :] == buckets[:, None, None], axis=2).astype(
        jnp.bfloat16
    )
    outgoing = jnp.dot(routing, normed, preferred_element_type=jnp.float32).astype(jnp.bfloat16)
    outgoing = outgoing.reshape(experts, capacity, model_width)
    partial_value = expert_block(
        lax.all_to_all(outgoing, "ep", split_axis=0, concat_axis=0, tiled=True),
        w_gate,
        w_up,
        w_down,
    )
    summed = lax.psum_scatter(
        partial_value.astype(jnp.float32).astype(jnp.bfloat16),
        "grp",
        scatter_dimension=2,
        tiled=True,
    ).astype(jnp.float32)
    returned = lax.all_to_all(
        summed.astype(jnp.bfloat16), "ep", split_axis=0, concat_axis=0, tiled=True
    ).astype(summed.dtype)
    feature_count = returned.shape[2]
    picked = returned.reshape(experts * capacity, feature_count)[positions]
    picked = picked.reshape(tok_rows, top_count, feature_count)
    result = jnp.sum(picked * mixing[:, :, None], axis=1)
    return result.astype(jnp.bfloat16)


def solution(mesh):
    return jax.shard_map(
        on_device,
        mesh=mesh,
        in_specs=(
            P("ep", None),
            P(),
            P("ep", None),
            P("ep", None),
            P("ep", "grp", None),
            P("ep", "grp", None),
            P("ep", "grp", None),
        ),
        out_specs=P("ep", "grp"),
        check_vma=False,
    )
```

profile of v0, /device:TPU:13, one launch (start us, length us, event | category | flops | bytes accessed | tf_op | source)
XLA Modules:
  0.0 456.0 jit_solution(7308030351800640279)
XLA Ops:
  6.5 0.0 reduce-scatter.2.cloned.1.call-start
  6.5 0.8 copy.15
  7.3 0.1 eq.42
  7.4 0.1 eq.38
  7.5 1.2 reduce-window.6
  8.7 0.2 slice_reduce_fusion
  8.9 0.1 fusion.17
  9.0 0.1 reduce_sum.41
  9.1 0.7 fusion.8
  9.8 1.2 fusion.9
  11.1 3.5 convolution_convert_fusion.1
  14.6 0.0 slice-start
  14.6 188.6 %all_to_all.10 = bf16[16,64,4096]{2,1,0:T(8,128)(2,1)S(1)} all-to-all(bf16[16,64,4096]{2,1,0:T(8,128)(2,1)S(1)} %bitcast.46), channel_id=1, replica_groups=mesh['grp'=2,'ep'=16] {'ep'}, dimensions={0} | all-to-all | bytes 16777216 | tf_op jit(solution)/shard_map/all_to_all | solution.py:44
  203.1 0.0 slice-start.1
  203.1 9.2 %fusion.1 = f32[1024,768]{1,0:T(8,128)S(1)} fusion(bf16[1024,4096]{1,0:T(8,128)(2,1)S(1)} %bitcast.48, bf16[1,768,4096]{2,1,0:T(8,128)(2,1)} %param.12), kind=kOutput, calls=%fused_computation.4 | convolution fusion | flops 6442450944 | bytes 17825792 | tf_op jit(solution)/shard_map/dot_general | solution.py:18
  212.3 0.0 slice-done
  212.3 0.0 slice-done.1
  212.3 7.0 %multiply_convert_fusion = bf16[1024,768]{1,0:T(8,128)(2,1)S(1)} fusion(f32[1024,768]{1,0:T(8,128)S(1)} %fusion.1, bf16[1024,4096]{1,0:T(8,128)(2,1)S(1)} %bitcast.49, bf16[1,768,4096]{2,1,0:T(8,128)(2,1)S(1)} %bitcast.53), kind=kOutput, calls=%fused_computation.11 | convolution fusion | flops 6447169536 | bytes 19398656 | tf_op jit(solution)/shard_map/dot_general | solution.py:17
  219.3 11.7 %convolution_convert_fusion = bf16[1024,4096]{1,0:T(8,128)(2,1)} fusion(bf16[1024,768]{1,0:T(8,128)(2,1)S(1)} %multiply_convert_fusion, bf16[1,768,4096]{2,1,0:T(8,128)(2,1)} %param.13), kind=kOutput, calls=%fused_computation.1 | convolution fusion | flops 6446645248 | bytes 16252928 | tf_op jit(solution)/shard_map/dot_general | solution.py:9
  231.0 0.0 reduce-scatter.2.cloned.1.call-update
  231.1 0.0 copy-start
  231.1 99.5 %reduce-scatter.2.cloned.1.call-done = bf16[16,64,2048]{2,1,0:T(8,128)(2,1)} async-done(((bf16[16,64,4096]{2,1,0:T(8,128)(2,1)}), bf16[16,64,2048]{2,1,0:T(8,128)(2,1)}) %reduce-scatter.2.cloned.1.call-update) | async-done | bytes 4194320 | tf_op jit(solution)/shard_map/reduce_scatter | solution.py:49
  330.6 6.5 %all-to-all-start.1 = ((bf16[16,64,2048]{2,1,0:T(8,128)(2,1)}), bf16[16,64,2048]{2,1,0:T(8,128)(2,1)}, u32[]{:S(2)}, u32[]{:S(2)}) async-start(bf16[16,64,2048]{2,1,0:T(8,128)(2,1)} %reduce-scatter.2.cloned.1.call-done), calls=%async_computation.2 | async-start | bytes 8388608 | tf_op jit(solution)/shard_map/all_to_all | solution.py:55
  337.1 0.1 mul.65
  337.2 0.0 copy-done
  337.2 0.1 copy.19
  337.3 92.2 %all-to-all-done.1 = bf16[16,64,2048]{2,1,0:T(8,128)(2,1)} async-done(((bf16[16,64,2048]{2,1,0:T(8,128)(2,1)}), bf16[16,64,2048]{2,1,0:T(8,128)(2,1)}, u32[]{:S(2)}, u32[]{:S(2)}) %all-to-all-start.1) | async-done | bytes 4194336 | tf_op jit(solution)/shard_map/all_to_all | solution.py:55
  429.6 6.5 %bitcast_convert_fusion = f32[1024,2048]{1,0:T(8,128)} fusion(bf16[16,64,2048]{2,1,0:T(8,128)(2,1)} %all-to-all-done.1), kind=kLoop, calls=%fused_computation.8 | loop fusion | flops 2097152 | bytes 12582912 | tf_op jit(solution)/shard_map/reshape | solution.py:59
  436.1 8.8 %gather_fusion = f32[512,2048]{1,0:T(8,128)} fusion(f32[1024,2048]{1,0:T(8,128)} %bitcast_convert_fusion, s32[1024]{0:T(1024)S(1)} %pad_clamp_fusion), kind=kCustom, calls=%fused_computation | custom fusion | bytes 8390656 | tf_op jit(solution)/shard_map/gather | solution.py:59
  444.8 4.4 fusion.5
  (10 shorter events, 0.1 us)
Async XLA Ops:
  6.5 324.1 %reduce-scatter.2.cloned.1.call-start = ((), (), s32[]{:S(2)}) async-start(), calls=%async_computation.3 | async-start | bytes 12582912 | tf_op jit(solution)/shard_map/reduce_scatter | solution.py:49
  14.6 197.7 %slice-start = ((s8[6291456]{0:T(1024)(128)(4,1)}), s8[2097152]{0:T(1024)(128)(4,1)S(1)}, s32[]{:S(2)}) async-start(s8[6291456]{0:T(1024)(128)(4,1)} %bitcast.52), calls=%async_computation.4 | async-start | bytes 4194304
  203.1 9.2 %slice-start.1 = ((s8[6291456]{0:T(1024)(128)(4,1)}), s8[4194304]{0:T(1024)(128)(4,1)S(1)}, s32[]{:S(2)}) async-start(s8[6291456]{0:T(1024)(128)(4,1)} %bitcast.52), calls=%async_computation.5 | async-start | bytes 8388608
  231.1 106.1 %copy-start = (f32[64,8]{0,1:T(8,128)S(1)}, f32[64,8]{0,1:T(8,128)}, u32[]{:S(2)}) copy-start(f32[64,8]{0,1:T(8,128)} %param.10) | copy-start | bytes 6148
  330.6 99.0 %all-to-all-start.1 = ((bf16[16,64,2048]{2,1,0:T(8,128)(2,1)}), bf16[16,64,2048]{2,1,0:T(8,128)(2,1)}, u32[]{:S(2)}, u32[]{:S(2)}) async-start(bf16[16,64,2048]{2,1,0:T(8,128)(2,1)} %reduce-scatter.2.cloned.1.call-done), calls=%async_computation.2 | async-start | bytes 8388608 | tf_op jit(solution)/shard_map/all_to_all | solution.py:55
Sparse Core Ops, SparseCore 0:
  231.2 99.3 reduce-scatter.1
where the time goes:
time: 456 us
  waiting for transfers between devices  192 us (42%)
  blocking collectives  189 us (41%)
  matrix products  31.3 us (7%)
  other arithmetic  14.1 us (3%)
  between operations  13.5 us (3%)
  local copies, waits for them, and re-layouts  10.2 us (2%)
  starting transfers between devices  6.49 us (1%)
    all_to_all x1, blocking collectives, on_device(): lax.all_to_all(outgoing, 'ep', split_axis=0, concat_axis=0, tiled=True)  189 us
    reduce_scatter x1, waiting for transfers between devices, on_device(): lax.psum_scatter(partial_value.astype(jnp.float32).astype(jnp.bfloat16),...  99.5 us
    all_to_all x1, waiting for transfers between devices, on_device(): lax.all_to_all(summed.astype(jnp.bfloat16), 'ep', split_axis=0, concat_ax...  92.2 us
    dot_general x1, matrix products, finish_expert(): jnp.dot(hidden, w_down[0], preferred_element_type=jnp.float32)  11.7 us
    dot_general x1, matrix products, expert_block(): lax.dot_general(flat_rows, w_up[0], contract, preferred_element_type=jnp....  9.16 us
  transfers between devices with their start and end apart: 2, of which 2 were waited for; matrix products, arithmetic and copies ran while one was open for 0% of the time, Pallas kernels for 0%

commit v1 on v0

--- a/solution.py
+++ b/solution.py
@@ -1,6 +1,10 @@
+import functools
+
 import jax
 import jax.numpy as jnp
 from jax import lax
+from jax.experimental import pallas as pl
+from jax.experimental.pallas import tpu as pltpu
 from jax.sharding import PartitionSpec as P
 
 
@@ -62,9 +66,288 @@
     return result.astype(jnp.bfloat16)
 
 
+MESH = pl.DeviceIdType.MESH
+LANES = 128
+CHUNKS = 2
+
+
+def tile_of(extent, most):
+    tile = most
+    while extent % tile:
+        tile //= 2
+    return tile
+
+
+def ring_kernel(
+    experts, x_ref, wg_ref, wu_ref, wd_ref, out_ref,
+    rows_in, wg, wu, wd, hidden, pair_out, pair_in, own, cross_out, cross_in, ring_out, ring_in,
+    gather_send, gather_recv, share_send, share_recv, pair_send, pair_recv,
+    cross_send, cross_recv, ring_send, ring_recv, load_sem,
+):
+    slots, both, _ = rows_in.shape
+    rows = both // 2
+    units, width = wg.shape
+    part = width // 2
+    half = slots // 2
+    me, grp = lax.axis_index("ep"), lax.axis_index("grp")
+    chip, core = me // 2, me % 2
+    column, level = chip % 2, chip // 2
+    place = level + column * (slots - 1 - 2 * level)
+
+    def at_place(p):
+        col = p // half
+        lev = p + col * (slots - 1 - 2 * p)
+        return (lev * 2 + col) * 2 + core
+
+    right = {"ep": at_place((place + 1) % slots)}
+    left = {"ep": at_place((place + slots - 1) % slots)}
+    partner = {"ep": chip * 2 + 1 - core}
+    across = {"grp": 1 - grp}
+
+    loads = [
+        pltpu.make_async_copy(x_ref, rows_in.at[0, pl.ds(0, rows)], load_sem.at[0]),
+        pltpu.make_async_copy(wg_ref.at[0], wg, load_sem.at[1]),
+        pltpu.make_async_copy(wu_ref.at[0], wu, load_sem.at[2]),
+        pltpu.make_async_copy(wd_ref.at[0], wd, load_sem.at[3]),
+    ]
+    for load in loads:
+        load.start()
+
+    barrier = pltpu.get_barrier_semaphore()
+    for other in (left, right, partner, across):
+        pl.semaphore_signal(barrier, inc=1, device_id=other, device_id_type=MESH)
+    pl.semaphore_wait(barrier, 4)
+
+    def remote(src, dst, send, recv, device):
+        return pltpu.make_async_remote_copy(
+            src_ref=src, dst_ref=dst, send_sem=send, recv_sem=recv, device_id=device, device_id_type=MESH
+        )
+
+    def slot_at(direction, distance):
+        if distance == 0:
+            return 0
+        if distance == half:
+            return slots - 1
+        return 2 * distance - 1 + direction
+
+    def block_slots(b):
+        if b == 0:
+            return 0, 1
+        if b == half:
+            return slots - 1, 1
+        return 2 * b - 1, 2
+
+    def gather_copy(direction, d):
+        source, target = slot_at(direction, d - 1), slot_at(direction, d)
+        span = pl.ds(0, rows)
+        if d == half:
+            span = pl.ds(direction * (rows // 2), rows // 2)
+        return remote(
+            rows_in.at[source, span], rows_in.at[target, span],
+            gather_send.at[direction, d - 1], gather_recv.at[direction, d - 1],
+            (right, left)[direction],
+        )
+
+    def share_copy(b):
+        first, count = block_slots(b)
+        return remote(
+            rows_in.at[pl.ds(first, count), pl.ds(0, rows)], rows_in.at[pl.ds(first, count), pl.ds(rows, rows)],
+            share_send.at[b], share_recv.at[b], partner,
+        )
+
+    def pair_copy(b):
+        span = pl.ds(*block_slots(b))
+        return remote(pair_out.at[span], pair_in.at[span], pair_send.at[b], pair_recv.at[b], partner)
+
+    def cross_copy(b):
+        span = pl.ds(*block_slots(b))
+        return remote(cross_out.at[span], cross_in.at[span], cross_send.at[b], cross_recv.at[b], across)
+
+    unit_tile = tile_of(units, 256)
+    col_tile = tile_of(part, 512)
+
+    def compute(b):
+        first, count = block_slots(b)
+        height = count * both
+        slab = pl.ds(first, count)
+        lanes = lax.broadcasted_iota(jnp.int32, (height, LANES), 1)
+        shares = rows_in[slab, :, pl.ds(width, LANES)].astype(jnp.float32).reshape(height, LANES)
+        weight = jnp.sum(
+            jnp.where((lanes == me) | (lanes == me + experts), shares, 0.0), axis=1, keepdims=True
+        )
+
+        def up_step(j, carry):
+            span = pl.ds(pl.multiple_of(j * unit_tile, unit_tile), unit_tile)
+            block = rows_in[slab, :, pl.ds(0, width)].reshape(height, width)
+            contract = (((1,), (1,)), ((), ()))
+            gate = lax.dot_general(block, wg[span, :], contract, preferred_element_type=jnp.float32)
+            upper = lax.dot_general(block, wu[span, :], contract, preferred_element_type=jnp.float32)
+            value = gate / (1.0 + jnp.exp(-gate)) * upper * weight
+            hidden[pl.ds(0, height), span] = value.astype(jnp.bfloat16)
+            return carry
+
+        lax.fori_loop(0, units // unit_tile, up_step, 0)
+        if b == 0:
+            loads[3].wait()
+
+        for h in range(2):
+            base = ((grp + 1 + h) % 2) * part
+
+            def down_step(j, carry):
+                held = pl.ds(pl.multiple_of(j * col_tile, col_tile), col_tile)
+                span = pl.ds(pl.multiple_of(base + j * col_tile, col_tile), col_tile)
+                value = jnp.dot(hidden[pl.ds(0, height), :], wd[:, span], preferred_element_type=jnp.float32)
+                value = value.reshape(count, 2, rows, col_tile)
+                own[h, slab, :, held] = value[:, 0]
+                pair_out[slab, h, :, held] = value[:, 1].astype(jnp.bfloat16)
+                return carry
+
+            lax.fori_loop(0, part // col_tile, down_step, 0)
+        pair_copy(b).start()
+
+    def add_pair(b):
+        first, count = block_slots(b)
+        pair_copy(b).wait_recv()
+        for s in range(first, first + count):
+            cross_out[s] = (own[0, s] + pair_in[s, 0].astype(jnp.float32)).astype(jnp.bfloat16)
+        cross_copy(b).start()
+        for s in range(first, first + count):
+            own[1, s] = own[1, s] + pair_in[s, 1].astype(jnp.float32)
+
+    def add_cross(b):
+        first, count = block_slots(b)
+        cross_copy(b).wait_recv()
+        for s in range(first, first + count):
+            own[1, s] = own[1, s] + cross_in[s].astype(jnp.float32)
+
+    loads[0].wait()
+    for b in range(half + 1):
+        if b > 0:
+            for direction in range(2):
+                gather_copy(direction, b).wait_recv()
+        if b < half:
+            for direction in range(2):
+                gather_copy(direction, b + 1).start()
+        share_copy(b).start()
+        share_copy(b).wait_recv()
+        if b == 0:
+            loads[1].wait()
+            loads[2].wait()
+        compute(b)
+        add_pair(b)
+        if b > 0:
+            add_cross(b - 1)
+    add_cross(half)
+
+    step_cols = part // CHUNKS
+
+    def ring_copy(direction, t, c):
+        span = pl.ds(0, rows)
+        if t == 0:
+            span = pl.ds(direction * (rows // 2), rows // 2)
+        return remote(
+            ring_out.at[direction, t, c, span], ring_in.at[direction, t, c, span],
+            ring_send.at[direction, t, c], ring_recv.at[direction, t, c],
+            (left, right)[direction],
+        )
+
+    for t in range(half):
+        for c in range(CHUNKS):
+            cols = pl.ds(c * step_cols, step_cols)
+            for direction in range(2):
+                slot = slot_at(direction, half - t)
+                if t > 0:
+                    ring_copy(direction, t - 1, c).wait_recv()
+                for piece in range(2):
+                    span = pl.ds(piece * (rows // 2), rows // 2)
+                    if t == 0 and piece != direction:
+                        continue
+                    value = own[1, slot, span, cols]
+                    if t > 1 or (t == 1 and piece == direction):
+                        value = value + ring_in[direction, t - 1, c, span].astype(jnp.float32)
+                    ring_out[direction, t, c, span] = value.astype(jnp.bfloat16)
+                ring_copy(direction, t, c).start()
+    for c in range(CHUNKS):
+        cols = pl.ds(c * step_cols, step_cols)
+        value = own[1, 0, :, cols]
+        for direction in range(2):
+            ring_copy(direction, half - 1, c).wait_recv()
+            value = value + ring_in[direction, half - 1, c].astype(jnp.float32)
+        out_ref[:, cols] = value.astype(out_ref.dtype)
+
+    for b in range(half + 1):
+        share_copy(b).wait_send()
+        pair_copy(b).wait_send()
+        cross_copy(b).wait_send()
+    for direction in range(2):
+        for d in range(half):
+            gather_copy(direction, d + 1).wait_send()
+            for c in range(CHUNKS):
+                ring_copy(direction, d, c).wait_send()
+
+
+def on_device_ring(tokens, norm_gain, expert_ids, gate_scores, w_gate, w_up, w_down):
+    experts = lax.axis_size("ep")
+    rows, width = tokens.shape
+    units = w_gate.shape[1]
+    slots = experts // 2
+    half = slots // 2
+    part = width // 2
+    floated = tokens.astype(jnp.float32)
+    scaled = lax.rsqrt(jnp.mean(floated * floated, axis=1, keepdims=True) + 1e-06)
+    normed = (floated * scaled * norm_gain[None, :]).astype(jnp.bfloat16)
+    mixing = gate_scores / jnp.sum(gate_scores, axis=1, keepdims=True)
+    chosen = expert_ids[:, :, None] == jnp.arange(experts, dtype=jnp.int32)[None, None, :]
+    dense = jnp.sum(jnp.where(chosen, mixing[:, :, None], 0.0), axis=1)
+    upper = lax.reduce_precision(dense, 8, 7)
+    shares = jnp.concatenate([upper, dense - upper], axis=1).astype(jnp.bfloat16)
+    shares = jnp.pad(shares, ((0, 0), (0, LANES - 2 * experts)))
+    packed = jnp.concatenate([normed, shares], axis=1)
+    dma = pltpu.SemaphoreType.DMA
+    bf16, f32 = jnp.bfloat16, jnp.float32
+    return pl.pallas_call(
+        functools.partial(ring_kernel, experts),
+        out_shape=jax.ShapeDtypeStruct((rows, part), bf16),
+        in_specs=[pl.BlockSpec(memory_space=pl.ANY)] * 4,
+        out_specs=pl.BlockSpec(memory_space=pltpu.VMEM),
+        scratch_shapes=[
+            pltpu.VMEM((slots, 2 * rows, width + LANES), bf16),
+            pltpu.VMEM((units, width), bf16),
+            pltpu.VMEM((units, width), bf16),
+            pltpu.VMEM((units, width), bf16),
+            pltpu.VMEM((4 * rows, units), bf16),
+            pltpu.VMEM((slots, 2, rows, part), bf16),
+            pltpu.VMEM((slots, 2, rows, part), bf16),
+            pltpu.VMEM((2, slots, rows, part), f32),
+            pltpu.VMEM((slots, rows, part), bf16),
+            pltpu.VMEM((slots, rows, part), bf16),
+            pltpu.VMEM((2, half, CHUNKS, rows, part // CHUNKS), bf16),
+            pltpu.VMEM((2, half, CHUNKS, rows, part // CHUNKS), bf16),
+            dma((2, half)), dma((2, half)),
+            dma((half + 1,)), dma((half + 1,)),
+            dma((half + 1,)), dma((half + 1,)),
+            dma((half + 1,)), dma((half + 1,)),
+            dma((2, half, CHUNKS)), dma((2, half, CHUNKS)),
+            dma((4,)),
+        ],
+        compiler_params=pltpu.CompilerParams(
+            collective_id=0, has_side_effects=True, vmem_limit_bytes=62 * 1024 * 1024
+        ),
+    )(packed, w_gate, w_up, w_down)
+
+
 def solution(mesh):
+    groups, experts = mesh.shape["grp"], mesh.shape["ep"]
+
+    def body(tokens, norm_gain, expert_ids, gate_scores, w_gate, w_up, w_down):
+        capacity = 2 * tokens.shape[0] * expert_ids.shape[1] // experts
+        whole_slabs = capacity >= tokens.shape[0] and w_gate.shape[0] == 1
+        ringable = groups == 2 and experts % 4 == 0 and experts >= 8 and 2 * experts <= LANES
+        chosen = on_device_ring if whole_slabs and ringable else on_device
+        return chosen(tokens, norm_gain, expert_ids, gate_scores, w_gate, w_up, w_down)
+
     return jax.shard_map(
-        on_device,
+        body,
         mesh=mesh,
         in_specs=(
             P("ep", None),

time: 456 us -> 104 us (0.23)
  the two profiles are of different devices: /device:TPU:13 before, /device:TPU:0 now
where the time goes in v1:
time: 104 us; the launch traced here: 103 us
  Pallas kernels  96 us (92%)
  other arithmetic  5.52 us (5%)
  local copies, waits for them, and re-layouts  1.84 us (2%)
    pallas_call x1, Pallas kernels, on_device_ring(): pl.pallas_call(functools.partial(ring_kernel, experts), out_shape=jax.Sha...  96 us

profile of v1, /device:TPU:0, one launch (start us, length us, event | category | flops | bytes accessed | tf_op | source)
XLA Modules:
  0.0 103.4 jit_solution(14847163272741563056)
XLA Ops:
  0.0 1.2 %fusion = f32[64]{0:T(128)S(1)} fusion(bf16[64,4096]{1,0:T(8,128)(2,1)} %param.7), kind=kLoop, calls=%fused_computation.2 | loop fusion | flops 786368 | bytes 524544 | tf_op jit(solution)/shard_map/reduce_sum | solution.py:297
  1.3 0.7 reduce_sum.28
  2.0 0.7 broadcast_divide_fusion
  2.7 0.7 select_reduce_fusion
  3.4 0.1 copy.13
  3.5 0.1 copy.12
  3.6 0.1 fusion.5
  3.6 1.2 %fusion.2 = bf16[64,4096]{1,0:T(8,128)(2,1)S(1)} fusion(bf16[64,4096]{1,0:T(8,128)(2,1)} %param.7, f32[4096]{0:T(1024)} %param.8, f32[64]{0:T(128)S(1)} %add_rsqrt_fusion), kind=kLoop, calls=%fused_computation.4 | loop fusion | flops 1048576 | bytes 1065216 | tf_op jit(solution)/shard_map/convert_element_type | solution.py:298
  4.9 0.8 pad_maximum_fusion.x_ref
  5.7 96.0 %shard_map.73 = bf16[64,2048]{1,0:T(8,128)(2,1)} custom-call(bf16[64,4224]{1,0:T(8,128)(2,1)} %pad_maximum_fusion.x_ref, bf16[1,768,4096]{2,1,0:T(8,128)(2,1)} %wg_ref.1, bf16[1,768,4096]{2,1,0:T(8,128)(2,1)} %wu_ref.1, bf16[1,768,4096]{2,1,0:T(8,128)(2,1)} %wd_ref.1), custom_call_target="tpu_custom_call" | custom-call | tf_op jit(solution)/shard_map/pallas_call | solution.py:308
  101.8 1.7 %copy.16 = bf16[64,2048]{1,0:T(8,128)(2,1)} copy(bf16[64,2048]{1,0:T(8,128)(2,1)} %shard_map.73) | data formatting | bytes 524288
  (3 shorter events, 0.0 us)

commit v2 on v1

--- a/solution.py
+++ b/solution.py
@@ -69,6 +69,7 @@
 MESH = pl.DeviceIdType.MESH
 LANES = 128
 CHUNKS = 2
+EARLY_SHARE = 4
 
 
 def tile_of(extent, most):
@@ -79,16 +80,19 @@
 
 
 def ring_kernel(
-    experts, x_ref, wg_ref, wu_ref, wd_ref, out_ref,
+    experts, tokens_ref, gain_ref, ids_ref, scores_ref, wg_ref, wu_ref, wd_ref, out_ref,
     rows_in, wg, wu, wd, hidden, pair_out, pair_in, own, cross_out, cross_in, ring_out, ring_in,
+    first_out, first_in, last_out, last_in,
     gather_send, gather_recv, share_send, share_recv, pair_send, pair_recv,
-    cross_send, cross_recv, ring_send, ring_recv, load_sem,
+    cross_send, cross_recv, ring_send, ring_recv, first_send, first_recv, last_sem, load_sem,
 ):
     slots, both, _ = rows_in.shape
     rows = both // 2
     units, width = wg.shape
     part = width // 2
     half = slots // 2
+    early = first_out.shape[-1]
+    late = part - early
     me, grp = lax.axis_index("ep"), lax.axis_index("grp")
     chip, core = me // 2, me % 2
     column, level = chip % 2, chip // 2
@@ -105,10 +109,9 @@
     across = {"grp": 1 - grp}
 
     loads = [
-        pltpu.make_async_copy(x_ref, rows_in.at[0, pl.ds(0, rows)], load_sem.at[0]),
-        pltpu.make_async_copy(wg_ref.at[0], wg, load_sem.at[1]),
-        pltpu.make_async_copy(wu_ref.at[0], wu, load_sem.at[2]),
-        pltpu.make_async_copy(wd_ref.at[0], wd, load_sem.at[3]),
+        pltpu.make_async_copy(wg_ref.at[0], wg, load_sem.at[0]),
+        pltpu.make_async_copy(wu_ref.at[0], wu, load_sem.at[1]),
+        pltpu.make_async_copy(wd_ref.at[0], wd, load_sem.at[2]),
     ]
     for load in loads:
         load.start()
@@ -116,6 +119,28 @@
     barrier = pltpu.get_barrier_semaphore()
     for other in (left, right, partner, across):
         pl.semaphore_signal(barrier, inc=1, device_id=other, device_id_type=MESH)
+
+    row_tile = tile_of(rows, 16)
+
+    def normalise(r, carry):
+        span = pl.ds(pl.multiple_of(r * row_tile, row_tile), row_tile)
+        floated = tokens_ref[span, :].astype(jnp.float32)
+        scaled = lax.rsqrt(jnp.mean(floated * floated, axis=1, keepdims=True) + 1e-06)
+        rows_in[0, span, pl.ds(0, width)] = (floated * scaled * gain_ref[...]).astype(jnp.bfloat16)
+        scores = scores_ref[span, :]
+        mixing = scores / jnp.sum(scores, axis=1, keepdims=True)
+        ids = ids_ref[span, :]
+        lanes = lax.broadcasted_iota(jnp.int32, (row_tile, LANES), 1)
+        upper = jnp.zeros((row_tile, LANES), jnp.float32)
+        lower = jnp.zeros((row_tile, LANES), jnp.float32)
+        for k in range(ids.shape[1]):
+            upper = jnp.where(lanes == ids[:, k:k + 1], mixing[:, k:k + 1], upper)
+            lower = jnp.where(lanes == ids[:, k:k + 1] + experts, mixing[:, k:k + 1], lower)
+        lower = lower - lower.astype(jnp.bfloat16).astype(jnp.float32)
+        rows_in[0, span, pl.ds(width, LANES)] = jnp.where(lanes < experts, upper, lower).astype(jnp.bfloat16)
+        return carry
+
+    lax.fori_loop(0, rows // row_tile, normalise, 0)
     pl.semaphore_wait(barrier, 4)
 
     def remote(src, dst, send, recv, device):
@@ -137,23 +162,42 @@
             return slots - 1, 1
         return 2 * b - 1, 2
 
-    def gather_copy(direction, d):
+    def gather_rows(direction, d, piece):
+        if d == half:
+            return direction * (rows // 2) + piece * (rows // 4), rows // 4
+        return (piece ^ direction) * (rows // 2), rows // 2
+
+    def gather_copy(direction, d, piece):
         source, target = slot_at(direction, d - 1), slot_at(direction, d)
-        span = pl.ds(0, rows)
-        if d == half:
-            span = pl.ds(direction * (rows // 2), rows // 2)
+        span = pl.ds(*gather_rows(direction, d, piece))
         return remote(
             rows_in.at[source, span], rows_in.at[target, span],
-            gather_send.at[direction, d - 1], gather_recv.at[direction, d - 1],
+            gather_send.at[direction, d - 1, piece], gather_recv.at[direction, d - 1, piece],
             (right, left)[direction],
         )
 
-    def share_copy(b):
-        first, count = block_slots(b)
+    def share_copy(direction, d, piece):
+        slot = slot_at(direction, d)
+        start, count = gather_rows(direction, d, piece)
         return remote(
-            rows_in.at[pl.ds(first, count), pl.ds(0, rows)], rows_in.at[pl.ds(first, count), pl.ds(rows, rows)],
-            share_send.at[b], share_recv.at[b], partner,
-        )
+            rows_in.at[slot, pl.ds(start, count)], rows_in.at[slot, pl.ds(rows + start, count)],
+            share_send.at[direction, d, piece], share_recv.at[direction, d, piece], partner,
+        )
+
+    def share_list(d):
+        if d == 0:
+            return [share_copy(0, 0, 0), share_copy(0, 0, 1)]
+        return [share_copy(direction, d, piece) for piece in range(2) for direction in range(2)]
+
+    def forward(d, piece):
+        for direction in range(2):
+            gather_copy(direction, d, piece).wait_recv()
+            if d + 1 < half:
+                gather_copy(direction, d + 1, piece).start()
+            elif d + 1 == half and piece == 0:
+                gather_copy(direction, half, 0).start()
+                gather_copy(direction, half, 1).start()
+            share_copy(direction, d, piece).start()
 
     def pair_copy(b):
         span = pl.ds(*block_slots(b))
@@ -187,8 +231,10 @@
             return carry
 
         lax.fori_loop(0, units // unit_tile, up_step, 0)
+        if b < half:
+            forward(b + 1, 0)
         if b == 0:
-            loads[3].wait()
+            loads[2].wait()
 
         for h in range(2):
             base = ((grp + 1 + h) % 2) * part
@@ -209,51 +255,79 @@
         first, count = block_slots(b)
         pair_copy(b).wait_recv()
         for s in range(first, first + count):
-            cross_out[s] = (own[0, s] + pair_in[s, 0].astype(jnp.float32)).astype(jnp.bfloat16)
+            total = own[0, s, :, pl.ds(early, late)] + pair_in[s, 0, :, pl.ds(early, late)].astype(jnp.float32)
+            cross_out[s] = total.astype(jnp.bfloat16)
         cross_copy(b).start()
         for s in range(first, first + count):
-            own[1, s] = own[1, s] + pair_in[s, 1].astype(jnp.float32)
+            own[0, s, :, pl.ds(0, early)] += pair_in[s, 0, :, pl.ds(0, early)].astype(jnp.float32)
+            own[1, s] += pair_in[s, 1].astype(jnp.float32)
 
     def add_cross(b):
         first, count = block_slots(b)
         cross_copy(b).wait_recv()
         for s in range(first, first + count):
-            own[1, s] = own[1, s] + cross_in[s].astype(jnp.float32)
-
-    loads[0].wait()
+            own[1, s, :, pl.ds(early, late)] += cross_in[s].astype(jnp.float32)
+
+    for piece in range(2):
+        for direction in range(2):
+            gather_copy(direction, 1, piece).start()
+    for copy in share_list(0):
+        copy.start()
     for b in range(half + 1):
         if b > 0:
-            for direction in range(2):
-                gather_copy(direction, b).wait_recv()
-        if b < half:
-            for direction in range(2):
-                gather_copy(direction, b + 1).start()
-        share_copy(b).start()
-        share_copy(b).wait_recv()
+            forward(b, 1)
+        for copy in share_list(b):
+            copy.wait_recv()
         if b == 0:
+            loads[0].wait()
             loads[1].wait()
-            loads[2].wait()
         compute(b)
         add_pair(b)
-        if b > 0:
-            add_cross(b - 1)
-    add_cross(half)
-
-    step_cols = part // CHUNKS
+        if b > 1:
+            add_cross(b - 2)
+
+    step_cols = late // CHUNKS
+
+    def ring_rows(direction, t):
+        return pl.ds(direction * (rows // 2), rows // 2) if t == 0 else pl.ds(0, rows)
 
     def ring_copy(direction, t, c):
-        span = pl.ds(0, rows)
-        if t == 0:
-            span = pl.ds(direction * (rows // 2), rows // 2)
+        span = ring_rows(direction, t)
         return remote(
             ring_out.at[direction, t, c, span], ring_in.at[direction, t, c, span],
             ring_send.at[direction, t, c], ring_recv.at[direction, t, c],
             (left, right)[direction],
         )
 
-    for t in range(half):
+    def first_copy(direction, t):
+        span = ring_rows(direction, t)
+        return remote(
+            first_out.at[direction, t, :, span], first_in.at[direction, t, :, span],
+            first_send.at[direction, t], first_recv.at[direction, t],
+            (left, right)[direction],
+        )
+
+    def last_copy():
+        return remote(last_out, last_in, last_sem.at[0], last_sem.at[1], across)
+
+    def first_step(t):
+        for direction in range(2):
+            slot = slot_at(direction, half - t)
+            if t > 0:
+                first_copy(direction, t - 1).wait_recv()
+            for piece in range(2):
+                span = pl.ds(piece * (rows // 2), rows // 2)
+                if t == 0 and piece != direction:
+                    continue
+                value = own[:, slot, span, pl.ds(0, early)]
+                if t > 1 or (t == 1 and piece == direction):
+                    value = value + first_in[direction, t - 1, :, span].astype(jnp.float32)
+                first_out[direction, t, :, span] = value.astype(jnp.bfloat16)
+            first_copy(direction, t).start()
+
+    def ring_step(t):
         for c in range(CHUNKS):
-            cols = pl.ds(c * step_cols, step_cols)
+            cols = pl.ds(early + c * step_cols, step_cols)
             for direction in range(2):
                 slot = slot_at(direction, half - t)
                 if t > 0:
@@ -267,21 +341,45 @@
                         value = value + ring_in[direction, t - 1, c, span].astype(jnp.float32)
                     ring_out[direction, t, c, span] = value.astype(jnp.bfloat16)
                 ring_copy(direction, t, c).start()
+
+    first_step(0)
+    add_cross(half - 1)
+    first_step(1)
+    add_cross(half)
+    for t in range(half):
+        ring_step(t)
+        if t + 2 < half:
+            first_step(t + 2)
+        elif t + 2 == half:
+            totals = own[:, 0, :, pl.ds(0, early)]
+            for direction in range(2):
+                first_copy(direction, half - 1).wait_recv()
+                totals = totals + first_in[direction, half - 1].astype(jnp.float32)
+            last_out[...] = totals[0].astype(jnp.bfloat16)
+            last_copy().start()
+            own[1, 0, :, pl.ds(0, early)] = totals[1]
+    last_copy().wait_recv()
+    head = own[1, 0, :, pl.ds(0, early)] + last_in[...].astype(jnp.float32)
+    out_ref[:, pl.ds(0, early)] = head.astype(out_ref.dtype)
     for c in range(CHUNKS):
-        cols = pl.ds(c * step_cols, step_cols)
+        cols = pl.ds(early + c * step_cols, step_cols)
         value = own[1, 0, :, cols]
         for direction in range(2):
             ring_copy(direction, half - 1, c).wait_recv()
             value = value + ring_in[direction, half - 1, c].astype(jnp.float32)
         out_ref[:, cols] = value.astype(out_ref.dtype)
 
+    last_copy().wait_send()
     for b in range(half + 1):
-        share_copy(b).wait_send()
+        for copy in share_list(b):
+            copy.wait_send()
         pair_copy(b).wait_send()
         cross_copy(b).wait_send()
     for direction in range(2):
         for d in range(half):
-            gather_copy(direction, d + 1).wait_send()
+            first_copy(direction, d).wait_send()
+            for piece in range(2):
+                gather_copy(direction, d + 1, piece).wait_send()
             for c in range(CHUNKS):
                 ring_copy(direction, d, c).wait_send()
 
@@ -293,22 +391,14 @@
     slots = experts // 2
     half = slots // 2
     part = width // 2
-    floated = tokens.astype(jnp.float32)
-    scaled = lax.rsqrt(jnp.mean(floated * floated, axis=1, keepdims=True) + 1e-06)
-    normed = (floated * scaled * norm_gain[None, :]).astype(jnp.bfloat16)
-    mixing = gate_scores / jnp.sum(gate_scores, axis=1, keepdims=True)
-    chosen = expert_ids[:, :, None] == jnp.arange(experts, dtype=jnp.int32)[None, None, :]
-    dense = jnp.sum(jnp.where(chosen, mixing[:, :, None], 0.0), axis=1)
-    upper = lax.reduce_precision(dense, 8, 7)
-    shares = jnp.concatenate([upper, dense - upper], axis=1).astype(jnp.bfloat16)
-    shares = jnp.pad(shares, ((0, 0), (0, LANES - 2 * experts)))
-    packed = jnp.concatenate([normed, shares], axis=1)
+    early = part // EARLY_SHARE
+    late = part - early
     dma = pltpu.SemaphoreType.DMA
     bf16, f32 = jnp.bfloat16, jnp.float32
     return pl.pallas_call(
         functools.partial(ring_kernel, experts),
         out_shape=jax.ShapeDtypeStruct((rows, part), bf16),
-        in_specs=[pl.BlockSpec(memory_space=pl.ANY)] * 4,
+        in_specs=[pl.BlockSpec(memory_space=pltpu.VMEM)] * 4 + [pl.BlockSpec(memory_space=pl.ANY)] * 3,
         out_specs=pl.BlockSpec(memory_space=pltpu.VMEM),
         scratch_shapes=[
             pltpu.VMEM((slots, 2 * rows, width + LANES), bf16),
@@ -319,21 +409,26 @@
             pltpu.VMEM((slots, 2, rows, part), bf16),
             pltpu.VMEM((slots, 2, rows, part), bf16),
             pltpu.VMEM((2, slots, rows, part), f32),
-            pltpu.VMEM((slots, rows, part), bf16),
-            pltpu.VMEM((slots, rows, part), bf16),
-            pltpu.VMEM((2, half, CHUNKS, rows, part // CHUNKS), bf16),
-            pltpu.VMEM((2, half, CHUNKS, rows, part // CHUNKS), bf16),
-            dma((2, half)), dma((2, half)),
-            dma((half + 1,)), dma((half + 1,)),
+            pltpu.VMEM((slots, rows, late), bf16),
+            pltpu.VMEM((slots, rows, late), bf16),
+            pltpu.VMEM((2, half, CHUNKS, rows, late // CHUNKS), bf16),
+            pltpu.VMEM((2, half, CHUNKS, rows, late // CHUNKS), bf16),
+            pltpu.VMEM((2, half, 2, rows, early), bf16),
+            pltpu.VMEM((2, half, 2, rows, early), bf16),
+            pltpu.VMEM((rows, early), bf16),
+            pltpu.VMEM((rows, early), bf16),
+            dma((2, half, 2)), dma((2, half, 2)),
+            dma((2, half + 1, 2)), dma((2, half + 1, 2)),
             dma((half + 1,)), dma((half + 1,)),
             dma((half + 1,)), dma((half + 1,)),
             dma((2, half, CHUNKS)), dma((2, half, CHUNKS)),
-            dma((4,)),
+            dma((2, half)), dma((2, half)), dma((2,)),
+            dma((3,)),
         ],
         compiler_params=pltpu.CompilerParams(
             collective_id=0, has_side_effects=True, vmem_limit_bytes=62 * 1024 * 1024
         ),
-    )(packed, w_gate, w_up, w_down)
+    )(tokens, norm_gain[None, :], expert_ids, gate_scores, w_gate, w_up, w_down)
 
 
 def solution(mesh):

time: 104 us -> 100 us (0.962)
  other arithmetic: 5.52 us -> 0 us
  local copies, waits for them, and re-layouts: 1.84 us -> 4.42 us
    unnamed x1 -> x3, local copies, waits for them, and re-layouts: 1.67 us -> 4.42 us
    reduce_sum x3 -> x0, other arithmetic: 2.67 us -> none  [the longest x1 1.24 us: on_device_ring(): jnp.mean(floated * floated, axis=1, keepdims=True) + 1e-06]
    convert_element_type x1 -> x0, other arithmetic: 1.23 us -> none  [on_device_ring(): normed = (floated * scaled * norm_gain[None, :]).astype(jnp.bfloat16)]
where the time goes in v2:
time: 100 us; the launch traced here: 99.9 us
  Pallas kernels  95.4 us (95%)
  local copies, waits for them, and re-layouts  4.42 us (4%)
    pallas_call x1, Pallas kernels, on_device_ring(): pl.pallas_call(functools.partial(ring_kernel, experts), out_shape=jax.Sha...  95.4 us
    unnamed x3, local copies, waits for them, and re-layouts  4.42 us

profile of v2, /device:TPU:0, one launch (start us, length us, event | category | flops | bytes accessed | tf_op | source)
XLA Modules:
  0.0 99.9 jit_solution(4723546880080535840)
XLA Ops:
  0.0 1.4 %copy.8.ids_ref = s32[64,8]{1,0:T(8,128)} copy(s32[64,8]{0,1:T(8,128)} %param.9) | data formatting | bytes 4096 | tf_op args[2]
  1.4 1.4 %copy.9.scores_ref = f32[64,8]{1,0:T(8,128)} copy(f32[64,8]{0,1:T(8,128)} %param.10) | data formatting | bytes 4096 | tf_op args[3]
  2.8 95.4 %shard_map.73 = bf16[64,2048]{1,0:T(8,128)(2,1)} custom-call(bf16[64,4096]{1,0:T(8,128)(2,1)} %tokens_ref.1, f32[1,4096]{1,0:T(1,128)} %bitcast.1, s32[64,8]{1,0:T(8,128)} %copy.8.ids_ref, f32[64,8]{1,0:T(8,128)} %copy.9.scores_ref, bf16[1,768,4096]{2,1,0:T(8,128)(2,1)} %wg_ref.1, bf16[1,768,4096]{2,1,0:T(8,128)(2,1)} %wu_ref.1, bf16[1,768,4096]{2,1,0:T(8,128)(2,1)} %wd_ref.1), custom_call_target="tpu_custom_call" | custom-call | tf_op jit(solution)/shard_map/pallas_call | solution.py:398
  98.2 1.7 %copy.11 = bf16[64,2048]{1,0:T(8,128)(2,1)} copy(bf16[64,2048]{1,0:T(8,128)(2,1)} %shard_map.73) | data formatting | bytes 524288
